TPU v7x, 512 devices: a whole 4x8x8 slice. The times are simulated.
512 devices in a mesh: seq: 32 (over x, z), exp: 16 (over y, core).
Axes of the slice: x: 4, y: 8, z: 8, core: 2. Of those that a mesh axis runs over, the one named last changes fastest.
Arguments:
- queries: bfloat16 [8192, 2048], P('seq', 'exp'), may hold values from -112 to 112
- key_rows: bfloat16 [8192, 2048], P('seq', 'exp'), may hold values from -4 to 4
- value_rows: bfloat16 [8192, 2048], P('seq', 'exp'), may hold values from -6 to 6
- out_grad: bfloat16 [8192, 2048], P('seq', 'exp'), may hold values from -6 to 6
- expert_ids: int32 [8192, 2], P('seq'), may hold values from 0 to 31, all different within a row
- gate_values: float32 [8192, 2], P('seq'), may hold values from 0.1 to 1
- alibi_slope: float32 [16], P('exp'), may hold values from 0.00012207031 to 0.1
- expert_in: bfloat16 [32, 2048, 4096], P('seq', None, 'exp'), may hold values from -0.125 to 0.125
- expert_out: bfloat16 [32, 4096, 2048], P('seq', 'exp'), may hold values from -0.09375 to 0.09375
Outputs:
- query_grad: bfloat16 [8192, 2048], P('seq', 'exp')
- key_grad: bfloat16 [8192, 2048], P('seq', 'exp')
- value_grad: bfloat16 [8192, 2048], P('seq', 'exp')
- expert_in_grad: bfloat16 [32, 2048, 4096], P('seq', None, 'exp')
- expert_out_grad: bfloat16 [32, 4096, 2048], P('seq', 'exp')
Inputs may be any that keep to these rules, and one draw needn't show every extreme that they name: `expert_ids`: each token names two different experts.
All inputs are finite; a program needn't handle non-finite values.
Results may differ from a plain program's by a relative error of at most 0.024.
Values may be sent and summed in bfloat16 or wider, within the bound.
A program may use at most 128 MiB of HBM per device.

v0:
```python
import jax
import jax.numpy as jnp
from jax import lax
from jax.sharding import PartitionSpec as P

HD = 128
WCH = 16


def shifted(block, axis, distance):
    devices = range(lax.axis_size(axis))
    route = [(i - distance, i) for i in devices if i - distance in devices]
    return lax.ppermute(block, axis, route)


def window_scores(query_heads, key_stack, slopes, seq_index, window):
    score_scale = HD ** (-0.5)
    block_len = query_heads.shape[0]
    raw_scores = (
        jnp.einsum("ihd,jhd->hij", query_heads, key_stack, preferred_element_type=jnp.float32)
        * score_scale
    )
    row_pos = lax.broadcasted_iota(jnp.int32, (block_len, key_stack.shape[0]), 0)
    col_pos = lax.broadcasted_iota(jnp.int32, (block_len, key_stack.shape[0]), 1)
    back_block = col_pos // block_len
    distance = row_pos - col_pos % block_len + back_block * block_len
    in_window = (distance >= 0) & (distance < window) & (seq_index - back_block >= 0)
    biased = raw_scores - slopes[:, None, None] * distance.astype(jnp.float32)[None]
    return jnp.where(in_window[None], biased, -jnp.inf)


def slot_routing(expert_ids, experts, capacity):
    flat_ids = jnp.concatenate([expert_ids[:, 0], expert_ids[:, 1]])
    entry_count = flat_ids.shape[0]
    expert_cols = lax.broadcasted_iota(jnp.int32, (entry_count, experts), 1)
    one_hot = (flat_ids[:, None] == expert_cols).astype(jnp.int32)
    before = jnp.cumsum(one_hot, axis=0) - one_hot
    position = jnp.sum(before * one_hot, axis=1)
    is_kept = position < capacity
    slot_index = flat_ids * capacity + position
    slot_rows = lax.broadcasted_iota(jnp.int32, (experts * capacity, entry_count), 0)
    return ((slot_rows == slot_index[None, :]) & is_kept[None, :]).astype(jnp.bfloat16)


def per_device(
    queries,
    key_rows,
    value_rows,
    out_grad,
    expert_ids,
    gate_values,
    alibi_slope,
    expert_in,
    expert_out,
):
    score_scale = HD ** (-0.5)
    block_len = queries.shape[0]
    features = queries.shape[1]
    head_count = features // HD
    seq_index = lax.axis_index("seq")
    stretches = WCH + 1
    window = WCH * block_len

    def relay_keys(step, carry):
        stack_keys, stack_values, current_keys, current_values = carry
        current_keys, current_values = shifted((current_keys, current_values), "seq", 1)
        stack_keys = lax.dynamic_update_index_in_dim(stack_keys, current_keys, step, 0)
        stack_values = lax.dynamic_update_index_in_dim(stack_values, current_values, step, 0)
        return (stack_keys, stack_values, current_keys, current_values)

    empty_stack = jnp.zeros((stretches, block_len, features), jnp.bfloat16)
    start_keys = lax.dynamic_update_index_in_dim(empty_stack, key_rows, 0, 0)
    start_values = lax.dynamic_update_index_in_dim(empty_stack, value_rows, 0, 0)
    key_stack, value_stack, unused_keys, unused_values = lax.fori_loop(
        1, stretches, relay_keys, (start_keys, start_values, key_rows, value_rows)
    )
    key_block = key_stack.reshape(stretches * block_len, head_count, HD)
    value_block = value_stack.reshape(stretches * block_len, head_count, HD)
    query_heads = queries.reshape(block_len, head_count, HD)
    scores = window_scores(query_heads, key_block, alibi_slope, seq_index, window)
    log_norm = jax.nn.logsumexp(scores, axis=2)
    probs_full = jnp.exp(scores - log_norm[:, :, None])
    weights = probs_full.astype(jnp.bfloat16)
    attn_heads = jnp.einsum(
        "hij,jhd->ihd", weights, value_block, preferred_element_type=jnp.float32
    ).astype(jnp.bfloat16)
    attn_out = attn_heads.reshape(block_len, features)
    experts = lax.axis_size("seq")
    capacity = 5 * block_len // (2 * experts)
    routing = slot_routing(expert_ids, experts, capacity)
    both_tokens = jnp.concatenate([attn_out, attn_out])
    scaled_grad = jnp.concatenate(
        [gate_values[:, 0:1] * out_grad, gate_values[:, 1:2] * out_grad]
    ).astype(jnp.bfloat16)
    send_tokens = jnp.dot(routing, both_tokens, preferred_element_type=jnp.float32).astype(
        jnp.bfloat16
    )
    send_grads = jnp.dot(routing, scaled_grad, preferred_element_type=jnp.float32).astype(
        jnp.bfloat16
    )
    recv_tokens, recv_grads = (
        lax.all_to_all(send_tokens, "seq", split_axis=0, concat_axis=0, tiled=True),
        lax.all_to_all(send_grads, "seq", split_axis=0, concat_axis=0, tiled=True),
    )
    weight_in = expert_in[0]
    weight_out = expert_out[0]
    full_tokens = lax.all_gather(recv_tokens, "exp", axis=1, tiled=True)
    pre_act = jnp.dot(full_tokens, weight_in, preferred_element_type=jnp.float32)
    full_grads = lax.all_gather(recv_grads, "exp", axis=1, tiled=True)
    logistic = jax.nn.sigmoid(pre_act)
    hidden = (pre_act * logistic).astype(jnp.bfloat16)
    through_out = lax.dot_general(
        full_grads, weight_out, (((1,), (1,)), ((), ())), preferred_element_type=jnp.float32
    )
    hidden_grad = (through_out * logistic * (1.0 + pre_act * (1.0 - logistic))).astype(jnp.bfloat16)
    out_weight_grad = lax.dot_general(
        hidden, full_grads, (((0,), (0,)), ((), ())), preferred_element_type=jnp.float32
    ).astype(jnp.bfloat16)
    in_weight_grad = lax.dot_general(
        full_tokens, hidden_grad, (((0,), (0,)), ((), ())), preferred_element_type=jnp.float32
    ).astype(jnp.bfloat16)
    back_rows = lax.psum_scatter(
        lax.dot_general(
            weight_in, hidden_grad, (((1,), (1,)), ((), ())), preferred_element_type=jnp.float32
        ).astype(jnp.bfloat16),
        "exp",
        scatter_dimension=0,
        tiled=True,
    )
    returned = lax.all_to_all(back_rows, "seq", split_axis=1, concat_axis=1, tiled=True)
    combined = lax.dot_general(
        routing, returned, (((0,), (1,)), ((), ())), preferred_element_type=jnp.float32
    )
    attn_grad = (out_grad.astype(jnp.float32) + combined[:block_len] + combined[block_len:]).astype(
        jnp.bfloat16
    )
    grad_heads = attn_grad.reshape(block_len, head_count, HD)
    row_delta = jnp.einsum(
        "ihd,ihd->hi", grad_heads, attn_heads, preferred_element_type=jnp.float32
    )
    dprob = jnp.einsum("ihd,jhd->hij", grad_heads, value_block, preferred_element_type=jnp.float32)
    dscore = (probs_full * (dprob - row_delta[:, :, None])).astype(jnp.bfloat16)
    query_grad = (
        jnp.einsum("hij,jhd->ihd", dscore, key_block, preferred_element_type=jnp.float32)
        * score_scale
    ).astype(jnp.bfloat16)
    key_parts = (
        jnp.einsum("hij,ihd->jhd", dscore, query_heads, preferred_element_type=jnp.float32)
        * score_scale
    ).reshape(stretches, block_len, features)
    value_parts = jnp.einsum(
        "hij,ihd->jhd", weights, grad_heads, preferred_element_type=jnp.float32
    ).reshape(stretches, block_len, features)

    def relay_grads(step, carry):
        key_acc, value_acc = carry
        key_acc, value_acc = (
            shifted(key_acc.astype(jnp.bfloat16), "seq", -1).astype(key_acc.dtype),
            shifted(value_acc.astype(jnp.bfloat16), "seq", -1).astype(value_acc.dtype),
        )
        index = stretches - 1 - step
        key_acc = key_acc + lax.dynamic_index_in_dim(key_parts, index, 0, keepdims=False)
        value_acc = value_acc + lax.dynamic_index_in_dim(value_parts, index, 0, keepdims=False)
        return (key_acc, value_acc)

    key_total, value_total = lax.fori_loop(
        1, stretches, relay_grads, (key_parts[stretches - 1], value_parts[stretches - 1])
    )
    key_grad = key_total.astype(jnp.bfloat16)
    value_grad = value_total.astype(jnp.bfloat16)
    return (
        query_grad.reshape(block_len, features),
        key_grad,
        value_grad,
        in_weight_grad[None],
        out_weight_grad[None],
    )


def solution(mesh):
    return jax.shard_map(
        per_device,
        mesh=mesh,
        in_specs=(
            P("seq", "exp"),
            P("seq", "exp"),
            P("seq", "exp"),
            P("seq", "exp"),
            P("seq", None),
            P("seq", None),
            P("exp"),
            P("seq", None, "exp"),
            P("seq", "exp", None),
        ),
        out_specs=(
            P("seq", "exp"),
            P("seq", "exp"),
            P("seq", "exp"),
            P("seq", None, "exp"),
            P("seq", "exp", None),
        ),
        check_vma=False,
    )
```

profile of v0, /device:TPU:2, one launch (start us, length us, event | category | flops | bytes accessed | tf_op | source)
XLA Modules:
  0.0 586.6 jit_solution(2084339012505833438)
XLA Ops:
  14.8 170.1 %while.36 = (s32[]{:T(128)}, bf16[17,256,128]{2,1,0:T(8,128)(2,1)S(1)}, bf16[17,256,128]{2,1,0:T(8,128)(2,1)S(1)}, bf16[256,128]{1,0:T(8,128)(2,1)S(1)}, bf16[25...) while((s32[]{:T(128)}, bf16[17,256,128]{2,1,0:T(8,128)(2,1)S(1)}, ...), condition=%wide.region_1.2_spmd, body=%wide.region_0.1_spmd.sunk | while | flops 5 | bytes 1048783 | solution.py:74
  14.8 4.3 collective-permute-start.1
  19.1 4.3 collective-permute-start
  23.4 4.6 collective-permute-done.1
  35.1 3.7 collective-permute-done.1
  42.1 3.8 collective-permute-start
  52.4 4.0 collective-permute-start
  62.6 3.7 collective-permute-start
  85.1 4.4 collective-permute-done.1
  95.3 4.4 collective-permute-done.1
  106.2 5.0 collective-permute-done.1
  117.0 4.4 collective-permute-done.1
  127.3 5.0 collective-permute-done.1
  137.5 4.8 collective-permute-done.1
  147.8 4.4 collective-permute-done.1
  158.0 4.4 collective-permute-done.1
  168.3 4.4 collective-permute-done.1
  178.5 4.4 collective-permute-done.1
  184.9 5.8 fusion.71
  194.7 15.8 %all_to_all.36 = bf16[32,20,128]{2,1,0:T(8,128)(2,1)} all-to-all(bf16[32,20,128]{2,1,0:T(8,128)(2,1)S(1)} %all_to_all.27), channel_id=1, replica_groups=mesh['seq'=32,'exp'=16] {'seq'}, dimensions={0} | all-to-all | bytes 327680 | tf_op jit(solution)/shard_map/all_to_all | solution.py:102
  215.3 15.9 %all_to_all.37 = bf16[32,20,128]{2,1,0:T(8,128)(2,1)} all-to-all(bf16[32,20,128]{2,1,0:T(8,128)(2,1)S(1)} %all_to_all.24), channel_id=1, replica_groups=mesh['seq'=32,'exp'=16] {'seq'}, dimensions={0} | all-to-all | bytes 327680 | tf_op jit(solution)/shard_map/all_to_all | solution.py:103
  232.9 22.8 %all-gather.5.cloned.1.call-done = bf16[640,2048]{1,0:T(8,128)(2,1)} async-done(((bf16[640,128]{1,0:T(8,128)(2,1)}), bf16[640,2048]{1,0:T(8,128)(2,1)}) %all-gather.5.cloned.1.call-update) | async-done | bytes 2621456 | tf_op jit(solution)/shard_map/all_gather | solution.py:107
  259.2 43.8 %all-gather.3.cloned.1.call-done = bf16[640,2048]{1,0:T(8,128)(2,1)} async-done(((bf16[640,128]{1,0:T(8,128)(2,1)}), bf16[640,2048]{1,0:T(8,128)(2,1)}) %all-gather.3.cloned.1.call-update) | async-done | bytes 2621456 | tf_op jit(solution)/shard_map/all_gather | solution.py:109
  309.2 4.4 copy.33
  313.6 4.0 fusion.14
  317.6 57.7 %reduce-scatter.4.cloned.1.call-done = bf16[128,640]{1,0:T(8,128)(2,1)} async-done(((bf16[2048,640]{1,0:T(8,128)(2,1)}), bf16[128,640]{1,0:T(8,128)(2,1)}) %reduce-scatter.4.cloned.1.call-update) | async-done | bytes 163856
  377.0 10.5 %all-to-all-start.2 = ((bf16[128,32,20]{0,2,1:T(8,128)(2,1)}), bf16[128,32,20]{0,2,1:T(8,128)(2,1)S(1)}, u32[]{:S(2)}, u32[]{:S(2)}) async-start(bf16[128,32,20]{0,2,1:T(8,128)(2,1)} %all_to_all.30), calls=%async_computation.2 | async-start | bytes 393216 | tf_op jit(solution)/shard_map/all_to_all | solution.py:130
  387.5 3.8 fusion.13
  391.3 5.7 all-to-all-done.2
  403.4 4.0 fusion.4
  412.9 166.5 %while.37 = (s32[]{:T(128)}, bf16[256,128]{1,0:T(8,128)(2,1)S(1)}, bf16[256,128]{1,0:T(8,128)(2,1)S(1)}, f32[17,256,128]{2,1,0:T(8,128)S(1)}, f32[17,256,128]{2,...) while((s32[]{:T(128)}, bf16[256,128]{1,0:T(8,128)(2,1)S(1)}, ...), condition=%wide.region_9.10_spmd, body=%wide.region_8.9_spmd.sunk | while | flops 196614 | bytes 1048803 | solution.py:166
  416.1 3.6 collective-permute-start.2
  422.3 5.7 collective-permute-start.3
  434.2 4.2 collective-permute-start.3
  444.6 4.0 collective-permute-start.3
  455.3 4.2 collective-permute-start.3
  465.7 4.0 collective-permute-start.3
  475.9 4.0 collective-permute-start.3
  486.2 4.0 collective-permute-start.3
  496.4 4.0 collective-permute-start.3
  506.6 4.0 collective-permute-start.3
  513.7 3.6 collective-permute-done.2
  517.3 3.6 collective-permute-start.3
  527.1 4.0 collective-permute-start.3
  537.3 4.6 collective-permute-start.3
  548.6 4.2 collective-permute-start.3
  559.0 4.0 collective-permute-start.3
  569.2 4.0 collective-permute-start.3
  (264 shorter events, 232.5 us)
Async XLA Ops:
  7.2 248.6 %all-gather.5.cloned.1.call-start = ((), (), s32[]{:S(2)}) async-start(), calls=%async_computation.5 | async-start | bytes 2785280 | tf_op jit(solution)/shard_map/all_gather | solution.py:107
  14.8 13.2 %collective-permute-start.1 = (bf16[256,128]{1,0:T(8,128)(2,1)S(1)}, bf16[256,128]{1,0:T(8,128)(2,1)S(1)}, u32[]{:S(2)}, u32[]{:S(2)}) collective-permute-start(bf16[256,128]{1,0:T(8,128)(2,1)S(1)} %get-tuple-element.375), channel_id=1, source_target_pairs={{0,16},{16,32},{32,48},{48,64},{64,80},{80,96},{96,112},{112,128},... | collective-permute-start | bytes 196616 | tf_op jit(solution)/shard_map/while/body/eval_jaxpr/ppermute | solution.py:13
  19.1 10.8 %collective-permute-start = (bf16[256,128]{1,0:T(8,128)(2,1)S(1)}, bf16[256,128]{1,0:T(8,128)(2,1)S(1)}, u32[]{:S(2)}, u32[]{:S(2)}) collective-permute-start(bf16[256,128]{1,0:T(8,128)(2,1)S(1)} %get-tuple-element.374), channel_id=1, source_target_pairs={{0,16},{16,32},{32,48},{48,64},{64,80},{80,96},{96,112},{112,128},... | collective-permute-start | bytes 196616 | tf_op jit(solution)/shard_map/while/body/eval_jaxpr/ppermute | solution.py:13
  30.0 8.9 %collective-permute-start.1 = (bf16[256,128]{1,0:T(8,128)(2,1)S(1)}, bf16[256,128]{1,0:T(8,128)(2,1)S(1)}, u32[]{:S(2)}, u32[]{:S(2)}) collective-permute-start(bf16[256,128]{1,0:T(8,128)(2,1)S(1)} %get-tuple-element.375), channel_id=1, source_target_pairs={{0,16},{16,32},{32,48},{48,64},{64,80},{80,96},{96,112},{112,128},... | collective-permute-start | bytes 196616 | tf_op jit(solution)/shard_map/while/body/eval_jaxpr/ppermute | solution.py:13
  31.9 8.3 %collective-permute-start = (bf16[256,128]{1,0:T(8,128)(2,1)S(1)}, bf16[256,128]{1,0:T(8,128)(2,1)S(1)}, u32[]{:S(2)}, u32[]{:S(2)}) collective-permute-start(bf16[256,128]{1,0:T(8,128)(2,1)S(1)} %get-tuple-element.374), channel_id=1, source_target_pairs={{0,16},{16,32},{32,48},{48,64},{64,80},{80,96},{96,112},{112,128},... | collective-permute-start | bytes 196616 | tf_op jit(solution)/shard_map/while/body/eval_jaxpr/ppermute | solution.py:13
  40.2 8.7 %collective-permute-start.1 = (bf16[256,128]{1,0:T(8,128)(2,1)S(1)}, bf16[256,128]{1,0:T(8,128)(2,1)S(1)}, u32[]{:S(2)}, u32[]{:S(2)}) collective-permute-start(bf16[256,128]{1,0:T(8,128)(2,1)S(1)} %get-tuple-element.375), channel_id=1, source_target_pairs={{0,16},{16,32},{32,48},{48,64},{64,80},{80,96},{96,112},{112,128},... | collective-permute-start | bytes 196616 | tf_op jit(solution)/shard_map/while/body/eval_jaxpr/ppermute | solution.py:13
  42.1 8.3 %collective-permute-start = (bf16[256,128]{1,0:T(8,128)(2,1)S(1)}, bf16[256,128]{1,0:T(8,128)(2,1)S(1)}, u32[]{:S(2)}, u32[]{:S(2)}) collective-permute-start(bf16[256,128]{1,0:T(8,128)(2,1)S(1)} %get-tuple-element.374), channel_id=1, source_target_pairs={{0,16},{16,32},{32,48},{48,64},{64,80},{80,96},{96,112},{112,128},... | collective-permute-start | bytes 196616 | tf_op jit(solution)/shard_map/while/body/eval_jaxpr/ppermute | solution.py:13
  50.5 8.3 %collective-permute-start.1 = (bf16[256,128]{1,0:T(8,128)(2,1)S(1)}, bf16[256,128]{1,0:T(8,128)(2,1)S(1)}, u32[]{:S(2)}, u32[]{:S(2)}) collective-permute-start(bf16[256,128]{1,0:T(8,128)(2,1)S(1)} %get-tuple-element.375), channel_id=1, source_target_pairs={{0,16},{16,32},{32,48},{48,64},{64,80},{80,96},{96,112},{112,128},... | collective-permute-start | bytes 196616 | tf_op jit(solution)/shard_map/while/body/eval_jaxpr/ppermute | solution.py:13
  52.4 8.3 %collective-permute-start = (bf16[256,128]{1,0:T(8,128)(2,1)S(1)}, bf16[256,128]{1,0:T(8,128)(2,1)S(1)}, u32[]{:S(2)}, u32[]{:S(2)}) collective-permute-start(bf16[256,128]{1,0:T(8,128)(2,1)S(1)} %get-tuple-element.374), channel_id=1, source_target_pairs={{0,16},{16,32},{32,48},{48,64},{64,80},{80,96},{96,112},{112,128},... | collective-permute-start | bytes 196616 | tf_op jit(solution)/shard_map/while/body/eval_jaxpr/ppermute | solution.py:13
  60.7 8.3 %collective-permute-start.1 = (bf16[256,128]{1,0:T(8,128)(2,1)S(1)}, bf16[256,128]{1,0:T(8,128)(2,1)S(1)}, u32[]{:S(2)}, u32[]{:S(2)}) collective-permute-start(bf16[256,128]{1,0:T(8,128)(2,1)S(1)} %get-tuple-element.375), channel_id=1, source_target_pairs={{0,16},{16,32},{32,48},{48,64},{64,80},{80,96},{96,112},{112,128},... | collective-permute-start | bytes 196616 | tf_op jit(solution)/shard_map/while/body/eval_jaxpr/ppermute | solution.py:13
  62.6 8.3 %collective-permute-start = (bf16[256,128]{1,0:T(8,128)(2,1)S(1)}, bf16[256,128]{1,0:T(8,128)(2,1)S(1)}, u32[]{:S(2)}, u32[]{:S(2)}) collective-permute-start(bf16[256,128]{1,0:T(8,128)(2,1)S(1)} %get-tuple-element.374), channel_id=1, source_target_pairs={{0,16},{16,32},{32,48},{48,64},{64,80},{80,96},{96,112},{112,128},... | collective-permute-start | bytes 196616 | tf_op jit(solution)/shard_map/while/body/eval_jaxpr/ppermute | solution.py:13
  71.0 8.3 %collective-permute-start.1 = (bf16[256,128]{1,0:T(8,128)(2,1)S(1)}, bf16[256,128]{1,0:T(8,128)(2,1)S(1)}, u32[]{:S(2)}, u32[]{:S(2)}) collective-permute-start(bf16[256,128]{1,0:T(8,128)(2,1)S(1)} %get-tuple-element.375), channel_id=1, source_target_pairs={{0,16},{16,32},{32,48},{48,64},{64,80},{80,96},{96,112},{112,128},... | collective-permute-start | bytes 196616 | tf_op jit(solution)/shard_map/while/body/eval_jaxpr/ppermute | solution.py:13
  72.9 8.3 %collective-permute-start = (bf16[256,128]{1,0:T(8,128)(2,1)S(1)}, bf16[256,128]{1,0:T(8,128)(2,1)S(1)}, u32[]{:S(2)}, u32[]{:S(2)}) collective-permute-start(bf16[256,128]{1,0:T(8,128)(2,1)S(1)} %get-tuple-element.374), channel_id=1, source_target_pairs={{0,16},{16,32},{32,48},{48,64},{64,80},{80,96},{96,112},{112,128},... | collective-permute-start | bytes 196616 | tf_op jit(solution)/shard_map/while/body/eval_jaxpr/ppermute | solution.py:13
  81.2 8.3 %collective-permute-start.1 = (bf16[256,128]{1,0:T(8,128)(2,1)S(1)}, bf16[256,128]{1,0:T(8,128)(2,1)S(1)}, u32[]{:S(2)}, u32[]{:S(2)}) collective-permute-start(bf16[256,128]{1,0:T(8,128)(2,1)S(1)} %get-tuple-element.375), channel_id=1, source_target_pairs={{0,16},{16,32},{32,48},{48,64},{64,80},{80,96},{96,112},{112,128},... | collective-permute-start | bytes 196616 | tf_op jit(solution)/shard_map/while/body/eval_jaxpr/ppermute | solution.py:13
  83.1 8.3 %collective-permute-start = (bf16[256,128]{1,0:T(8,128)(2,1)S(1)}, bf16[256,128]{1,0:T(8,128)(2,1)S(1)}, u32[]{:S(2)}, u32[]{:S(2)}) collective-permute-start(bf16[256,128]{1,0:T(8,128)(2,1)S(1)} %get-tuple-element.374), channel_id=1, source_target_pairs={{0,16},{16,32},{32,48},{48,64},{64,80},{80,96},{96,112},{112,128},... | collective-permute-start | bytes 196616 | tf_op jit(solution)/shard_map/while/body/eval_jaxpr/ppermute | solution.py:13
  91.5 8.3 %collective-permute-start.1 = (bf16[256,128]{1,0:T(8,128)(2,1)S(1)}, bf16[256,128]{1,0:T(8,128)(2,1)S(1)}, u32[]{:S(2)}, u32[]{:S(2)}) collective-permute-start(bf16[256,128]{1,0:T(8,128)(2,1)S(1)} %get-tuple-element.375), channel_id=1, source_target_pairs={{0,16},{16,32},{32,48},{48,64},{64,80},{80,96},{96,112},{112,128},... | collective-permute-start | bytes 196616 | tf_op jit(solution)/shard_map/while/body/eval_jaxpr/ppermute | solution.py:13
  93.4 8.9 %collective-permute-start = (bf16[256,128]{1,0:T(8,128)(2,1)S(1)}, bf16[256,128]{1,0:T(8,128)(2,1)S(1)}, u32[]{:S(2)}, u32[]{:S(2)}) collective-permute-start(bf16[256,128]{1,0:T(8,128)(2,1)S(1)} %get-tuple-element.374), channel_id=1, source_target_pairs={{0,16},{16,32},{32,48},{48,64},{64,80},{80,96},{96,112},{112,128},... | collective-permute-start | bytes 196616 | tf_op jit(solution)/shard_map/while/body/eval_jaxpr/ppermute | solution.py:13
  102.3 8.9 %collective-permute-start.1 = (bf16[256,128]{1,0:T(8,128)(2,1)S(1)}, bf16[256,128]{1,0:T(8,128)(2,1)S(1)}, u32[]{:S(2)}, u32[]{:S(2)}) collective-permute-start(bf16[256,128]{1,0:T(8,128)(2,1)S(1)} %get-tuple-element.375), channel_id=1, source_target_pairs={{0,16},{16,32},{32,48},{48,64},{64,80},{80,96},{96,112},{112,128},... | collective-permute-start | bytes 196616 | tf_op jit(solution)/shard_map/while/body/eval_jaxpr/ppermute | solution.py:13
  104.2 8.9 %collective-permute-start = (bf16[256,128]{1,0:T(8,128)(2,1)S(1)}, bf16[256,128]{1,0:T(8,128)(2,1)S(1)}, u32[]{:S(2)}, u32[]{:S(2)}) collective-permute-start(bf16[256,128]{1,0:T(8,128)(2,1)S(1)} %get-tuple-element.374), channel_id=1, source_target_pairs={{0,16},{16,32},{32,48},{48,64},{64,80},{80,96},{96,112},{112,128},... | collective-permute-start | bytes 196616 | tf_op jit(solution)/shard_map/while/body/eval_jaxpr/ppermute | solution.py:13
  113.2 8.3 %collective-permute-start.1 = (bf16[256,128]{1,0:T(8,128)(2,1)S(1)}, bf16[256,128]{1,0:T(8,128)(2,1)S(1)}, u32[]{:S(2)}, u32[]{:S(2)}) collective-permute-start(bf16[256,128]{1,0:T(8,128)(2,1)S(1)} %get-tuple-element.375), channel_id=1, source_target_pairs={{0,16},{16,32},{32,48},{48,64},{64,80},{80,96},{96,112},{112,128},... | collective-permute-start | bytes 196616 | tf_op jit(solution)/shard_map/while/body/eval_jaxpr/ppermute | solution.py:13
  115.1 8.3 %collective-permute-start = (bf16[256,128]{1,0:T(8,128)(2,1)S(1)}, bf16[256,128]{1,0:T(8,128)(2,1)S(1)}, u32[]{:S(2)}, u32[]{:S(2)}) collective-permute-start(bf16[256,128]{1,0:T(8,128)(2,1)S(1)} %get-tuple-element.374), channel_id=1, source_target_pairs={{0,16},{16,32},{32,48},{48,64},{64,80},{80,96},{96,112},{112,128},... | collective-permute-start | bytes 196616 | tf_op jit(solution)/shard_map/while/body/eval_jaxpr/ppermute | solution.py:13
  123.4 8.9 %collective-permute-start.1 = (bf16[256,128]{1,0:T(8,128)(2,1)S(1)}, bf16[256,128]{1,0:T(8,128)(2,1)S(1)}, u32[]{:S(2)}, u32[]{:S(2)}) collective-permute-start(bf16[256,128]{1,0:T(8,128)(2,1)S(1)} %get-tuple-element.375), channel_id=1, source_target_pairs={{0,16},{16,32},{32,48},{48,64},{64,80},{80,96},{96,112},{112,128},... | collective-permute-start | bytes 196616 | tf_op jit(solution)/shard_map/while/body/eval_jaxpr/ppermute | solution.py:13
  125.4 8.3 %collective-permute-start = (bf16[256,128]{1,0:T(8,128)(2,1)S(1)}, bf16[256,128]{1,0:T(8,128)(2,1)S(1)}, u32[]{:S(2)}, u32[]{:S(2)}) collective-permute-start(bf16[256,128]{1,0:T(8,128)(2,1)S(1)} %get-tuple-element.374), channel_id=1, source_target_pairs={{0,16},{16,32},{32,48},{48,64},{64,80},{80,96},{96,112},{112,128},... | collective-permute-start | bytes 196616 | tf_op jit(solution)/shard_map/while/body/eval_jaxpr/ppermute | solution.py:13
  133.7 8.7 %collective-permute-start.1 = (bf16[256,128]{1,0:T(8,128)(2,1)S(1)}, bf16[256,128]{1,0:T(8,128)(2,1)S(1)}, u32[]{:S(2)}, u32[]{:S(2)}) collective-permute-start(bf16[256,128]{1,0:T(8,128)(2,1)S(1)} %get-tuple-element.375), channel_id=1, source_target_pairs={{0,16},{16,32},{32,48},{48,64},{64,80},{80,96},{96,112},{112,128},... | collective-permute-start | bytes 196616 | tf_op jit(solution)/shard_map/while/body/eval_jaxpr/ppermute | solution.py:13
  135.6 8.3 %collective-permute-start = (bf16[256,128]{1,0:T(8,128)(2,1)S(1)}, bf16[256,128]{1,0:T(8,128)(2,1)S(1)}, u32[]{:S(2)}, u32[]{:S(2)}) collective-permute-start(bf16[256,128]{1,0:T(8,128)(2,1)S(1)} %get-tuple-element.374), channel_id=1, source_target_pairs={{0,16},{16,32},{32,48},{48,64},{64,80},{80,96},{96,112},{112,128},... | collective-permute-start | bytes 196616 | tf_op jit(solution)/shard_map/while/body/eval_jaxpr/ppermute | solution.py:13
  143.9 8.3 %collective-permute-start.1 = (bf16[256,128]{1,0:T(8,128)(2,1)S(1)}, bf16[256,128]{1,0:T(8,128)(2,1)S(1)}, u32[]{:S(2)}, u32[]{:S(2)}) collective-permute-start(bf16[256,128]{1,0:T(8,128)(2,1)S(1)} %get-tuple-element.375), channel_id=1, source_target_pairs={{0,16},{16,32},{32,48},{48,64},{64,80},{80,96},{96,112},{112,128},... | collective-permute-start | bytes 196616 | tf_op jit(solution)/shard_map/while/body/eval_jaxpr/ppermute | solution.py:13
  145.9 8.3 %collective-permute-start = (bf16[256,128]{1,0:T(8,128)(2,1)S(1)}, bf16[256,128]{1,0:T(8,128)(2,1)S(1)}, u32[]{:S(2)}, u32[]{:S(2)}) collective-permute-start(bf16[256,128]{1,0:T(8,128)(2,1)S(1)} %get-tuple-element.374), channel_id=1, source_target_pairs={{0,16},{16,32},{32,48},{48,64},{64,80},{80,96},{96,112},{112,128},... | collective-permute-start | bytes 196616 | tf_op jit(solution)/shard_map/while/body/eval_jaxpr/ppermute | solution.py:13
  154.2 8.3 %collective-permute-start.1 = (bf16[256,128]{1,0:T(8,128)(2,1)S(1)}, bf16[256,128]{1,0:T(8,128)(2,1)S(1)}, u32[]{:S(2)}, u32[]{:S(2)}) collective-permute-start(bf16[256,128]{1,0:T(8,128)(2,1)S(1)} %get-tuple-element.375), channel_id=1, source_target_pairs={{0,16},{16,32},{32,48},{48,64},{64,80},{80,96},{96,112},{112,128},... | collective-permute-start | bytes 196616 | tf_op jit(solution)/shard_map/while/body/eval_jaxpr/ppermute | solution.py:13
  156.1 8.3 %collective-permute-start = (bf16[256,128]{1,0:T(8,128)(2,1)S(1)}, bf16[256,128]{1,0:T(8,128)(2,1)S(1)}, u32[]{:S(2)}, u32[]{:S(2)}) collective-permute-start(bf16[256,128]{1,0:T(8,128)(2,1)S(1)} %get-tuple-element.374), channel_id=1, source_target_pairs={{0,16},{16,32},{32,48},{48,64},{64,80},{80,96},{96,112},{112,128},... | collective-permute-start | bytes 196616 | tf_op jit(solution)/shard_map/while/body/eval_jaxpr/ppermute | solution.py:13
  164.4 8.3 %collective-permute-start.1 = (bf16[256,128]{1,0:T(8,128)(2,1)S(1)}, bf16[256,128]{1,0:T(8,128)(2,1)S(1)}, u32[]{:S(2)}, u32[]{:S(2)}) collective-permute-start(bf16[256,128]{1,0:T(8,128)(2,1)S(1)} %get-tuple-element.375), channel_id=1, source_target_pairs={{0,16},{16,32},{32,48},{48,64},{64,80},{80,96},{96,112},{112,128},... | collective-permute-start | bytes 196616 | tf_op jit(solution)/shard_map/while/body/eval_jaxpr/ppermute | solution.py:13
  166.4 8.3 %collective-permute-start = (bf16[256,128]{1,0:T(8,128)(2,1)S(1)}, bf16[256,128]{1,0:T(8,128)(2,1)S(1)}, u32[]{:S(2)}, u32[]{:S(2)}) collective-permute-start(bf16[256,128]{1,0:T(8,128)(2,1)S(1)} %get-tuple-element.374), channel_id=1, source_target_pairs={{0,16},{16,32},{32,48},{48,64},{64,80},{80,96},{96,112},{112,128},... | collective-permute-start | bytes 196616 | tf_op jit(solution)/shard_map/while/body/eval_jaxpr/ppermute | solution.py:13
  174.7 8.3 %collective-permute-start.1 = (bf16[256,128]{1,0:T(8,128)(2,1)S(1)}, bf16[256,128]{1,0:T(8,128)(2,1)S(1)}, u32[]{:S(2)}, u32[]{:S(2)}) collective-permute-start(bf16[256,128]{1,0:T(8,128)(2,1)S(1)} %get-tuple-element.375), channel_id=1, source_target_pairs={{0,16},{16,32},{32,48},{48,64},{64,80},{80,96},{96,112},{112,128},... | collective-permute-start | bytes 196616 | tf_op jit(solution)/shard_map/while/body/eval_jaxpr/ppermute | solution.py:13
  176.6 8.3 %collective-permute-start = (bf16[256,128]{1,0:T(8,128)(2,1)S(1)}, bf16[256,128]{1,0:T(8,128)(2,1)S(1)}, u32[]{:S(2)}, u32[]{:S(2)}) collective-permute-start(bf16[256,128]{1,0:T(8,128)(2,1)S(1)} %get-tuple-element.374), channel_id=1, source_target_pairs={{0,16},{16,32},{32,48},{48,64},{64,80},{80,96},{96,112},{112,128},... | collective-permute-start | bytes 196616 | tf_op jit(solution)/shard_map/while/body/eval_jaxpr/ppermute | solution.py:13
  212.2 90.8 %all-gather.3.cloned.1.call-start = ((), (), s32[]{:S(2)}) async-start(), calls=%async_computation.4 | async-start | bytes 2785280 | tf_op jit(solution)/shard_map/all_gather | solution.py:109
  232.9 142.4 %reduce-scatter.4.cloned.1.call-start = ((), (), s32[]{:S(2)}) async-start(), calls=%async_computation.6 | async-start | bytes 2785280
  377.0 20.0 %all-to-all-start.2 = ((bf16[128,32,20]{0,2,1:T(8,128)(2,1)}), bf16[128,32,20]{0,2,1:T(8,128)(2,1)S(1)}, u32[]{:S(2)}, u32[]{:S(2)}) async-start(bf16[128,32,20]{0,2,1:T(8,128)(2,1)} %all_to_all.30), calls=%async_computation.2 | async-start | bytes 393216 | tf_op jit(solution)/shard_map/all_to_all | solution.py:130
  412.9 6.8 %collective-permute-start.3 = (bf16[256,128]{1,0:T(8,128)(2,1)S(1)}, bf16[256,128]{1,0:T(8,128)(2,1)S(1)}, u32[]{:S(2)}, u32[]{:S(2)}) collective-permute-start(bf16[256,128]{1,0:T(8,128)(2,1)S(1)} %get-tuple-element.398), channel_id=1, source_target_pairs={{16,0},{32,16},{48,32},{64,48},{80,64},{96,80},{112,96},{128,112},... | collective-permute-start | bytes 196616 | tf_op jit(solution)/shard_map/while/body/eval_jaxpr/ppermute | solution.py:13
  422.3 7.7 %collective-permute-start.3 = (bf16[256,128]{1,0:T(8,128)(2,1)S(1)}, bf16[256,128]{1,0:T(8,128)(2,1)S(1)}, u32[]{:S(2)}, u32[]{:S(2)}) collective-permute-start(bf16[256,128]{1,0:T(8,128)(2,1)S(1)} %get-tuple-element.398), channel_id=1, source_target_pairs={{16,0},{32,16},{48,32},{64,48},{80,64},{96,80},{112,96},{128,112},... | collective-permute-start | bytes 196616 | tf_op jit(solution)/shard_map/while/body/eval_jaxpr/ppermute | solution.py:13
  428.0 6.2 %collective-permute-start.2 = (bf16[256,128]{1,0:T(8,128)(2,1)S(1)}, bf16[256,128]{1,0:T(8,128)(2,1)S(1)}, u32[]{:S(2)}, u32[]{:S(2)}) collective-permute-start(bf16[256,128]{1,0:T(8,128)(2,1)S(1)} %get-tuple-element.397), channel_id=1, source_target_pairs={{16,0},{32,16},{48,32},{64,48},{80,64},{96,80},{112,96},{128,112},... | collective-permute-start | bytes 196616 | tf_op jit(solution)/shard_map/while/body/eval_jaxpr/ppermute | solution.py:13
  434.2 6.2 %collective-permute-start.3 = (bf16[256,128]{1,0:T(8,128)(2,1)S(1)}, bf16[256,128]{1,0:T(8,128)(2,1)S(1)}, u32[]{:S(2)}, u32[]{:S(2)}) collective-permute-start(bf16[256,128]{1,0:T(8,128)(2,1)S(1)} %get-tuple-element.398), channel_id=1, source_target_pairs={{16,0},{32,16},{48,32},{64,48},{80,64},{96,80},{112,96},{128,112},... | collective-permute-start | bytes 196616 | tf_op jit(solution)/shard_map/while/body/eval_jaxpr/ppermute | solution.py:13
  444.6 6.6 %collective-permute-start.3 = (bf16[256,128]{1,0:T(8,128)(2,1)S(1)}, bf16[256,128]{1,0:T(8,128)(2,1)S(1)}, u32[]{:S(2)}, u32[]{:S(2)}) collective-permute-start(bf16[256,128]{1,0:T(8,128)(2,1)S(1)} %get-tuple-element.398), channel_id=1, source_target_pairs={{16,0},{32,16},{48,32},{64,48},{80,64},{96,80},{112,96},{128,112},... | collective-permute-start | bytes 196616 | tf_op jit(solution)/shard_map/while/body/eval_jaxpr/ppermute | solution.py:13
  448.6 6.6 %collective-permute-start.2 = (bf16[256,128]{1,0:T(8,128)(2,1)S(1)}, bf16[256,128]{1,0:T(8,128)(2,1)S(1)}, u32[]{:S(2)}, u32[]{:S(2)}) collective-permute-start(bf16[256,128]{1,0:T(8,128)(2,1)S(1)} %get-tuple-element.397), channel_id=1, source_target_pairs={{16,0},{32,16},{48,32},{64,48},{80,64},{96,80},{112,96},{128,112},... | collective-permute-start | bytes 196616 | tf_op jit(solution)/shard_map/while/body/eval_jaxpr/ppermute | solution.py:13
  465.7 6.4 %collective-permute-start.3 = (bf16[256,128]{1,0:T(8,128)(2,1)S(1)}, bf16[256,128]{1,0:T(8,128)(2,1)S(1)}, u32[]{:S(2)}, u32[]{:S(2)}) collective-permute-start(bf16[256,128]{1,0:T(8,128)(2,1)S(1)} %get-tuple-element.398), channel_id=1, source_target_pairs={{16,0},{32,16},{48,32},{64,48},{80,64},{96,80},{112,96},{128,112},... | collective-permute-start | bytes 196616 | tf_op jit(solution)/shard_map/while/body/eval_jaxpr/ppermute | solution.py:13
  475.9 6.2 %collective-permute-start.3 = (bf16[256,128]{1,0:T(8,128)(2,1)S(1)}, bf16[256,128]{1,0:T(8,128)(2,1)S(1)}, u32[]{:S(2)}, u32[]{:S(2)}) collective-permute-start(bf16[256,128]{1,0:T(8,128)(2,1)S(1)} %get-tuple-element.398), channel_id=1, source_target_pairs={{16,0},{32,16},{48,32},{64,48},{80,64},{96,80},{112,96},{128,112},... | collective-permute-start | bytes 196616 | tf_op jit(solution)/shard_map/while/body/eval_jaxpr/ppermute | solution.py:13
  496.4 6.8 %collective-permute-start.3 = (bf16[256,128]{1,0:T(8,128)(2,1)S(1)}, bf16[256,128]{1,0:T(8,128)(2,1)S(1)}, u32[]{:S(2)}, u32[]{:S(2)}) collective-permute-start(bf16[256,128]{1,0:T(8,128)(2,1)S(1)} %get-tuple-element.398), channel_id=1, source_target_pairs={{16,0},{32,16},{48,32},{64,48},{80,64},{96,80},{112,96},{128,112},... | collective-permute-start | bytes 196616 | tf_op jit(solution)/shard_map/while/body/eval_jaxpr/ppermute | solution.py:13
  510.7 6.6 %collective-permute-start.2 = (bf16[256,128]{1,0:T(8,128)(2,1)S(1)}, bf16[256,128]{1,0:T(8,128)(2,1)S(1)}, u32[]{:S(2)}, u32[]{:S(2)}) collective-permute-start(bf16[256,128]{1,0:T(8,128)(2,1)S(1)} %get-tuple-element.397), channel_id=1, source_target_pairs={{16,0},{32,16},{48,32},{64,48},{80,64},{96,80},{112,96},{128,112},... | collective-permute-start | bytes 196616 | tf_op jit(solution)/shard_map/while/body/eval_jaxpr/ppermute | solution.py:13
  537.3 7.0 %collective-permute-start.3 = (bf16[256,128]{1,0:T(8,128)(2,1)S(1)}, bf16[256,128]{1,0:T(8,128)(2,1)S(1)}, u32[]{:S(2)}, u32[]{:S(2)}) collective-permute-start(bf16[256,128]{1,0:T(8,128)(2,1)S(1)} %get-tuple-element.398), channel_id=1, source_target_pairs={{16,0},{32,16},{48,32},{64,48},{80,64},{96,80},{112,96},{128,112},... | collective-permute-start | bytes 196616 | tf_op jit(solution)/shard_map/while/body/eval_jaxpr/ppermute | solution.py:13
  541.9 6.7 %collective-permute-start.2 = (bf16[256,128]{1,0:T(8,128)(2,1)S(1)}, bf16[256,128]{1,0:T(8,128)(2,1)S(1)}, u32[]{:S(2)}, u32[]{:S(2)}) collective-permute-start(bf16[256,128]{1,0:T(8,128)(2,1)S(1)} %get-tuple-element.397), channel_id=1, source_target_pairs={{16,0},{32,16},{48,32},{64,48},{80,64},{96,80},{112,96},{128,112},... | collective-permute-start | bytes 196616 | tf_op jit(solution)/shard_map/while/body/eval_jaxpr/ppermute | solution.py:13
  (30 other events, 405.7 us)
Sparse Core Ops, SparseCore 0:
  212.3 43.3 all-gather.4
  258.4 44.5 all-gather.2
  313.7 61.4 reduce-scatter.3
where the time goes:
time: 590 us; the launch traced here: 587 us
  waiting for transfers between devices  277 us (47%)
  starting transfers between devices  183 us (31%)
  matrix products  35.4 us (6%)
  blocking collectives  31.8 us (5%)
  local copies, waits for them, and re-layouts  21.9 us (4%)
  other arithmetic  21.3 us (4%)
  between operations  14.7 us (2%)
    ppermute x64, starting transfers between devices, shifted(): return lax.ppermute(block, axis, route)  173 us
    ppermute x64, waiting for transfers between devices, shifted(): return lax.ppermute(block, axis, route)  147 us
    unnamed x4, waiting for transfers between devices  57.7 us
    all_gather x1, waiting for transfers between devices, per_device(): full_grads = lax.all_gather(recv_grads, 'exp', axis=1, tiled=True)  43.8 us
    all_gather x1, waiting for transfers between devices, per_device(): full_tokens = lax.all_gather(recv_tokens, 'exp', axis=1, tiled=True)  22.8 us
    all_to_all x1, blocking collectives, per_device(): lax.all_to_all(send_grads, 'seq', split_axis=0, concat_axis=0, tiled=True)  15.9 us
    all_to_all x1, blocking collectives, per_device(): lax.all_to_all(send_tokens, 'seq', split_axis=0, concat_axis=0, tiled=True)  15.8 us
    add x16, other arithmetic, relay_grads(): value_acc + lax.dynamic_index_in_dim(value_parts, index, 0, keepdims=False)  14.7 us
  transfers between devices with their start and end apart: 68, of which 64 were waited for; matrix products, arithmetic and copies ran while one was open for 5% of the time, Pallas kernels for 0%

commit v1 on v0

--- a/solution.py
+++ b/solution.py
@@ -5,6 +5,17 @@
 
 HD = 128
 WCH = 16
+
+
+def pass_along(x, axis, along):
+    n_dev = lax.axis_size(axis)
+    right = [(i, (i + 1) % n_dev) for i in range(n_dev)]
+    terms = [x]
+    for far in range(1, n_dev):
+        terms = [lax.ppermute(terms[0], axis, right), *terms]
+    result = jnp.concatenate(terms, axis=along)
+    shift = (lax.axis_index(axis) + 1) * terms[-1].shape[along]
+    return jnp.roll(result, shift, axis=along)
 
 
 def shifted(block, axis, distance):
@@ -104,7 +115,7 @@
     )
     weight_in = expert_in[0]
     weight_out = expert_out[0]
-    full_tokens = lax.all_gather(recv_tokens, "exp", axis=1, tiled=True)
+    full_tokens = pass_along(recv_tokens, "exp", 1)
     pre_act = jnp.dot(full_tokens, weight_in, preferred_element_type=jnp.float32)
     full_grads = lax.all_gather(recv_grads, "exp", axis=1, tiled=True)
     logistic = jax.nn.sigmoid(pre_act)

time: 590 us -> 628 us (1.064)
  waiting for transfers between devices: 277 us -> 315 us
  blocking collectives: 31.8 us -> 15.6 us
  local copies, waits for them, and re-layouts: 21.9 us -> 36.9 us
    ppermute x0 -> x15, waiting for transfers between devices: none -> 83.1 us  [pass_along(): terms = [lax.ppermute(terms[0], axis, right), *terms]]
    all_gather x1, waiting for transfers between devices: 43.8 us -> 0.02 us  [per_device(): full_grads = lax.all_gather(recv_grads, 'exp', axis=1, tiled=True)]
    all_gather x1 -> x0, waiting for transfers between devices: 22.8 us -> none  [per_device(): full_tokens = lax.all_gather(recv_tokens, 'exp', axis=1, tiled=True)]
    unnamed x26 -> x73, local copies, waits for them, and re-layouts: 10 us -> 28.4 us
    all_to_all x1 -> x0, blocking collectives: 15.9 us -> none  [per_device(): lax.all_to_all(send_grads, 'seq', split_axis=0, concat_axis=0, tiled=True)]
    ppermute x64, waiting for transfers between devices: 147 us -> 161 us  [shifted(): return lax.ppermute(block, axis, route)]
    unnamed x4 -> x3, waiting for transfers between devices: 57.7 us -> 62.5 us
  transfers between devices with their start and end apart: 68 -> 83, of which waited for: 64 -> 76; matrix products, arithmetic and copies ran while one was open for 5% -> 4% of each run, Pallas kernels for 0% -> 0%
where the time goes in v1:
time: 628 us; the launch traced here: 625 us
  waiting for transfers between devices  315 us (50%)
  starting transfers between devices  189 us (30%)
  local copies, waits for them, and re-layouts  36.9 us (6%)
  matrix products  31 us (5%)
  other arithmetic  20.4 us (3%)
  blocking collectives  15.6 us (2%)
  between operations  15.3 us (2%)
    ppermute x64, starting transfers between devices, shifted(): return lax.ppermute(block, axis, route)  172 us
    ppermute x64, waiting for transfers between devices, shifted(): return lax.ppermute(block, axis, route)  161 us
    ppermute x15, waiting for transfers between devices, pass_along(): terms = [lax.ppermute(terms[0], axis, right), *terms]  83.1 us
    unnamed x3, waiting for transfers between devices  62.5 us
    unnamed x73, local copies, waits for them, and re-layouts  28.4 us
    all_to_all x1, blocking collectives, per_device(): lax.all_to_all(send_tokens, 'seq', split_axis=0, concat_axis=0, tiled=True)  15.6 us
    add x16, other arithmetic, relay_grads(): value_acc + lax.dynamic_index_in_dim(value_parts, index, 0, keepdims=False)  14.7 us
  transfers between devices with their start and end apart: 83, of which 76 were waited for; matrix products, arithmetic and copies ran while one was open for 4% of the time, Pallas kernels for 0%

profile of v1, /device:TPU:2, one launch (start us, length us, event | category | flops | bytes accessed | tf_op | source)
XLA Modules:
  0.0 624.7 jit_solution(6289347989920543827)
XLA Ops:
  14.7 170.1 %while.36 = (s32[]{:T(128)}, bf16[17,256,128]{2,1,0:T(8,128)(2,1)S(1)}, bf16[17,256,128]{2,1,0:T(8,128)(2,1)S(1)}, bf16[256,128]{1,0:T(8,128)(2,1)S(1)}, bf16[25...) while((s32[]{:T(128)}, bf16[17,256,128]{2,1,0:T(8,128)(2,1)S(1)}, ...), condition=%wide.region_1.2_spmd, body=%wide.region_0.1_spmd.sunk | while | flops 5 | bytes 1048791 | solution.py:85
  14.7 4.3 collective-permute-start
  19.0 4.3 collective-permute-start.1
  23.3 4.6 collective-permute-done
  85.0 4.4 collective-permute-done
  95.2 4.4 collective-permute-done
  106.1 5.0 collective-permute-done
  116.9 4.4 collective-permute-done
  127.2 5.0 collective-permute-done
  137.4 4.8 collective-permute-done
  147.7 4.4 collective-permute-done
  157.9 4.4 collective-permute-done
  168.2 4.4 collective-permute-done
  178.4 4.4 collective-permute-done
  184.8 6.0 fusion.74
  194.0 15.6 %all_to_all.36 = bf16[32,20,128]{2,1,0:T(8,128)(2,1)S(1)} all-to-all(bf16[32,20,128]{2,1,0:T(8,128)(2,1)S(1)} %all_to_all.27), channel_id=1, replica_groups=mesh['seq'=32,'exp'=16] {'seq'}, dimensions={0} | all-to-all | bytes 327680 | tf_op jit(solution)/shard_map/all_to_all | solution.py:113
  209.7 5.9 collective-permute-done.4
  215.7 6.0 collective-permute-done.5
  221.6 6.0 collective-permute-done.6
  227.6 6.0 collective-permute-done.7
  233.5 6.0 collective-permute-done.8
  239.5 5.9 collective-permute-done.9
  246.4 5.1 collective-permute-done.10
  252.6 5.4 all-to-all-start
  258.1 6.3 %collective-permute-done.12 = bf16[640,128]{1,0:T(8,128)(2,1)} collective-permute-done((bf16[640,128]{1,0:T(8,128)(2,1)}, bf16[640,128]{1,0:T(8,128)(2,1)}, u32[]{:S(2)}, u32[]{:S(2)}) %collective-permute-start.12) | collective-permute-done | bytes 163872 | tf_op jit(solution)/shard_map/ppermute | solution.py:15
  270.7 6.2 collective-permute-done.14
  276.8 6.0 collective-permute-done.15
  283.4 7.7 %collective-permute-done.16 = bf16[640,128]{1,0:T(8,128)(2,1)S(1)} collective-permute-done((bf16[640,128]{1,0:T(8,128)(2,1)S(1)}, bf16[640,128]{1,0:T(8,128)(2,1)S(1)}, u32[]{:S(2)}, u32[]{:S(2)}) %collective-permute-start.16) | collective-permute-done | bytes 163872 | tf_op jit(solution)/shard_map/ppermute | solution.py:15
  291.8 6.9 %collective-permute-done.17 = bf16[640,128]{1,0:T(8,128)(2,1)} collective-permute-done((bf16[640,128]{1,0:T(8,128)(2,1)S(1)}, bf16[640,128]{1,0:T(8,128)(2,1)}, u32[]{:S(2)}, u32[]{:S(2)}) %collective-permute-start.17) | collective-permute-done | bytes 163872 | tf_op jit(solution)/shard_map/ppermute | solution.py:15
  298.8 7.0 %collective-permute-done.18 = bf16[640,128]{1,0:T(8,128)(2,1)} collective-permute-done((bf16[640,128]{1,0:T(8,128)(2,1)}, bf16[640,128]{1,0:T(8,128)(2,1)}, u32[]{:S(2)}, u32[]{:S(2)}) %collective-permute-start.18) | collective-permute-done | bytes 163872 | tf_op jit(solution)/shard_map/ppermute | solution.py:15
  329.0 4.4 copy.33
  337.2 62.5 %reduce-scatter.4.cloned.1.call-done = bf16[128,640]{1,0:T(8,128)(2,1)} async-done(((bf16[2048,640]{1,0:T(8,128)(2,1)}), bf16[128,640]{1,0:T(8,128)(2,1)}) %reduce-scatter.4.cloned.1.call-update) | async-done | bytes 163856
  401.5 10.5 %all-to-all-start.2 = ((bf16[128,32,20]{0,2,1:T(8,128)(2,1)}), bf16[128,32,20]{0,2,1:T(8,128)(2,1)S(1)}, u32[]{:S(2)}, u32[]{:S(2)}) async-start(bf16[128,32,20]{0,2,1:T(8,128)(2,1)} %all_to_all.30), calls=%async_computation.2 | async-start | bytes 393216 | tf_op jit(solution)/shard_map/all_to_all | solution.py:141
  415.7 5.7 all-to-all-done.2
  422.1 4.6 convolution_bitcast_fusion
  436.7 180.5 %while.37 = (s32[]{:T(128)}, bf16[256,128]{1,0:T(8,128)(2,1)S(1)}, bf16[256,128]{1,0:T(8,128)(2,1)S(1)}, f32[17,256,128]{2,1,0:T(8,128)S(1)}, f32[17,256,128]{2,...) while((s32[]{:T(128)}, bf16[256,128]{1,0:T(8,128)(2,1)S(1)}, ...), condition=%wide.region_9.10_spmd, body=%wide.region_8.9_spmd.sunk | while | flops 196614 | bytes 1048803 | solution.py:177
  447.4 5.4 collective-permute-start.2
  454.7 4.2 collective-permute-done.3
  459.9 4.0 collective-permute-start.2
  471.0 4.5 collective-permute-start.2
  477.4 4.5 collective-permute-done.3
  493.7 4.3 collective-permute-start.2
  500.0 4.2 collective-permute-done.3
  544.7 4.3 collective-permute-done.3
  571.9 4.2 collective-permute-start.2
  578.1 4.2 collective-permute-done.3
  594.8 4.2 collective-permute-start.2
  601.0 4.1 collective-permute-done.3
  (340 shorter events, 301.6 us)
Async XLA Ops:
  14.7 13.2 %collective-permute-start = (bf16[256,128]{1,0:T(8,128)(2,1)S(1)}, bf16[256,128]{1,0:T(8,128)(2,1)S(1)}, u32[]{:S(2)}, u32[]{:S(2)}) collective-permute-start(bf16[256,128]{1,0:T(8,128)(2,1)S(1)} %get-tuple-element.374), channel_id=1, source_target_pairs={{0,16},{16,32},{32,48},{48,64},{64,80},{80,96},{96,112},{112,128},... | collective-permute-start | bytes 196616 | tf_op jit(solution)/shard_map/while/body/eval_jaxpr/ppermute | solution.py:24
  19.0 10.8 %collective-permute-start.1 = (bf16[256,128]{1,0:T(8,128)(2,1)S(1)}, bf16[256,128]{1,0:T(8,128)(2,1)S(1)}, u32[]{:S(2)}, u32[]{:S(2)}) collective-permute-start(bf16[256,128]{1,0:T(8,128)(2,1)S(1)} %get-tuple-element.375), channel_id=1, source_target_pairs={{0,16},{16,32},{32,48},{48,64},{64,80},{80,96},{96,112},{112,128},... | collective-permute-start | bytes 196616 | tf_op jit(solution)/shard_map/while/body/eval_jaxpr/ppermute | solution.py:24
  29.9 8.9 %collective-permute-start = (bf16[256,128]{1,0:T(8,128)(2,1)S(1)}, bf16[256,128]{1,0:T(8,128)(2,1)S(1)}, u32[]{:S(2)}, u32[]{:S(2)}) collective-permute-start(bf16[256,128]{1,0:T(8,128)(2,1)S(1)} %get-tuple-element.374), channel_id=1, source_target_pairs={{0,16},{16,32},{32,48},{48,64},{64,80},{80,96},{96,112},{112,128},... | collective-permute-start | bytes 196616 | tf_op jit(solution)/shard_map/while/body/eval_jaxpr/ppermute | solution.py:24
  31.8 8.3 %collective-permute-start.1 = (bf16[256,128]{1,0:T(8,128)(2,1)S(1)}, bf16[256,128]{1,0:T(8,128)(2,1)S(1)}, u32[]{:S(2)}, u32[]{:S(2)}) collective-permute-start(bf16[256,128]{1,0:T(8,128)(2,1)S(1)} %get-tuple-element.375), channel_id=1, source_target_pairs={{0,16},{16,32},{32,48},{48,64},{64,80},{80,96},{96,112},{112,128},... | collective-permute-start | bytes 196616 | tf_op jit(solution)/shard_map/while/body/eval_jaxpr/ppermute | solution.py:24
  40.1 8.7 %collective-permute-start = (bf16[256,128]{1,0:T(8,128)(2,1)S(1)}, bf16[256,128]{1,0:T(8,128)(2,1)S(1)}, u32[]{:S(2)}, u32[]{:S(2)}) collective-permute-start(bf16[256,128]{1,0:T(8,128)(2,1)S(1)} %get-tuple-element.374), channel_id=1, source_target_pairs={{0,16},{16,32},{32,48},{48,64},{64,80},{80,96},{96,112},{112,128},... | collective-permute-start | bytes 196616 | tf_op jit(solution)/shard_map/while/body/eval_jaxpr/ppermute | solution.py:24
  42.0 8.3 %collective-permute-start.1 = (bf16[256,128]{1,0:T(8,128)(2,1)S(1)}, bf16[256,128]{1,0:T(8,128)(2,1)S(1)}, u32[]{:S(2)}, u32[]{:S(2)}) collective-permute-start(bf16[256,128]{1,0:T(8,128)(2,1)S(1)} %get-tuple-element.375), channel_id=1, source_target_pairs={{0,16},{16,32},{32,48},{48,64},{64,80},{80,96},{96,112},{112,128},... | collective-permute-start | bytes 196616 | tf_op jit(solution)/shard_map/while/body/eval_jaxpr/ppermute | solution.py:24
  50.4 8.3 %collective-permute-start = (bf16[256,128]{1,0:T(8,128)(2,1)S(1)}, bf16[256,128]{1,0:T(8,128)(2,1)S(1)}, u32[]{:S(2)}, u32[]{:S(2)}) collective-permute-start(bf16[256,128]{1,0:T(8,128)(2,1)S(1)} %get-tuple-element.374), channel_id=1, source_target_pairs={{0,16},{16,32},{32,48},{48,64},{64,80},{80,96},{96,112},{112,128},... | collective-permute-start | bytes 196616 | tf_op jit(solution)/shard_map/while/body/eval_jaxpr/ppermute | solution.py:24
  52.3 8.3 %collective-permute-start.1 = (bf16[256,128]{1,0:T(8,128)(2,1)S(1)}, bf16[256,128]{1,0:T(8,128)(2,1)S(1)}, u32[]{:S(2)}, u32[]{:S(2)}) collective-permute-start(bf16[256,128]{1,0:T(8,128)(2,1)S(1)} %get-tuple-element.375), channel_id=1, source_target_pairs={{0,16},{16,32},{32,48},{48,64},{64,80},{80,96},{96,112},{112,128},... | collective-permute-start | bytes 196616 | tf_op jit(solution)/shard_map/while/body/eval_jaxpr/ppermute | solution.py:24
  60.6 8.3 %collective-permute-start = (bf16[256,128]{1,0:T(8,128)(2,1)S(1)}, bf16[256,128]{1,0:T(8,128)(2,1)S(1)}, u32[]{:S(2)}, u32[]{:S(2)}) collective-permute-start(bf16[256,128]{1,0:T(8,128)(2,1)S(1)} %get-tuple-element.374), channel_id=1, source_target_pairs={{0,16},{16,32},{32,48},{48,64},{64,80},{80,96},{96,112},{112,128},... | collective-permute-start | bytes 196616 | tf_op jit(solution)/shard_map/while/body/eval_jaxpr/ppermute | solution.py:24
  62.5 8.3 %collective-permute-start.1 = (bf16[256,128]{1,0:T(8,128)(2,1)S(1)}, bf16[256,128]{1,0:T(8,128)(2,1)S(1)}, u32[]{:S(2)}, u32[]{:S(2)}) collective-permute-start(bf16[256,128]{1,0:T(8,128)(2,1)S(1)} %get-tuple-element.375), channel_id=1, source_target_pairs={{0,16},{16,32},{32,48},{48,64},{64,80},{80,96},{96,112},{112,128},... | collective-permute-start | bytes 196616 | tf_op jit(solution)/shard_map/while/body/eval_jaxpr/ppermute | solution.py:24
  70.9 8.3 %collective-permute-start = (bf16[256,128]{1,0:T(8,128)(2,1)S(1)}, bf16[256,128]{1,0:T(8,128)(2,1)S(1)}, u32[]{:S(2)}, u32[]{:S(2)}) collective-permute-start(bf16[256,128]{1,0:T(8,128)(2,1)S(1)} %get-tuple-element.374), channel_id=1, source_target_pairs={{0,16},{16,32},{32,48},{48,64},{64,80},{80,96},{96,112},{112,128},... | collective-permute-start | bytes 196616 | tf_op jit(solution)/shard_map/while/body/eval_jaxpr/ppermute | solution.py:24
  72.8 8.3 %collective-permute-start.1 = (bf16[256,128]{1,0:T(8,128)(2,1)S(1)}, bf16[256,128]{1,0:T(8,128)(2,1)S(1)}, u32[]{:S(2)}, u32[]{:S(2)}) collective-permute-start(bf16[256,128]{1,0:T(8,128)(2,1)S(1)} %get-tuple-element.375), channel_id=1, source_target_pairs={{0,16},{16,32},{32,48},{48,64},{64,80},{80,96},{96,112},{112,128},... | collective-permute-start | bytes 196616 | tf_op jit(solution)/shard_map/while/body/eval_jaxpr/ppermute | solution.py:24
  81.1 8.3 %collective-permute-start = (bf16[256,128]{1,0:T(8,128)(2,1)S(1)}, bf16[256,128]{1,0:T(8,128)(2,1)S(1)}, u32[]{:S(2)}, u32[]{:S(2)}) collective-permute-start(bf16[256,128]{1,0:T(8,128)(2,1)S(1)} %get-tuple-element.374), channel_id=1, source_target_pairs={{0,16},{16,32},{32,48},{48,64},{64,80},{80,96},{96,112},{112,128},... | collective-permute-start | bytes 196616 | tf_op jit(solution)/shard_map/while/body/eval_jaxpr/ppermute | solution.py:24
  83.1 8.3 %collective-permute-start.1 = (bf16[256,128]{1,0:T(8,128)(2,1)S(1)}, bf16[256,128]{1,0:T(8,128)(2,1)S(1)}, u32[]{:S(2)}, u32[]{:S(2)}) collective-permute-start(bf16[256,128]{1,0:T(8,128)(2,1)S(1)} %get-tuple-element.375), channel_id=1, source_target_pairs={{0,16},{16,32},{32,48},{48,64},{64,80},{80,96},{96,112},{112,128},... | collective-permute-start | bytes 196616 | tf_op jit(solution)/shard_map/while/body/eval_jaxpr/ppermute | solution.py:24
  91.4 8.3 %collective-permute-start = (bf16[256,128]{1,0:T(8,128)(2,1)S(1)}, bf16[256,128]{1,0:T(8,128)(2,1)S(1)}, u32[]{:S(2)}, u32[]{:S(2)}) collective-permute-start(bf16[256,128]{1,0:T(8,128)(2,1)S(1)} %get-tuple-element.374), channel_id=1, source_target_pairs={{0,16},{16,32},{32,48},{48,64},{64,80},{80,96},{96,112},{112,128},... | collective-permute-start | bytes 196616 | tf_op jit(solution)/shard_map/while/body/eval_jaxpr/ppermute | solution.py:24
  93.3 8.9 %collective-permute-start.1 = (bf16[256,128]{1,0:T(8,128)(2,1)S(1)}, bf16[256,128]{1,0:T(8,128)(2,1)S(1)}, u32[]{:S(2)}, u32[]{:S(2)}) collective-permute-start(bf16[256,128]{1,0:T(8,128)(2,1)S(1)} %get-tuple-element.375), channel_id=1, source_target_pairs={{0,16},{16,32},{32,48},{48,64},{64,80},{80,96},{96,112},{112,128},... | collective-permute-start | bytes 196616 | tf_op jit(solution)/shard_map/while/body/eval_jaxpr/ppermute | solution.py:24
  102.2 8.9 %collective-permute-start = (bf16[256,128]{1,0:T(8,128)(2,1)S(1)}, bf16[256,128]{1,0:T(8,128)(2,1)S(1)}, u32[]{:S(2)}, u32[]{:S(2)}) collective-permute-start(bf16[256,128]{1,0:T(8,128)(2,1)S(1)} %get-tuple-element.374), channel_id=1, source_target_pairs={{0,16},{16,32},{32,48},{48,64},{64,80},{80,96},{96,112},{112,128},... | collective-permute-start | bytes 196616 | tf_op jit(solution)/shard_map/while/body/eval_jaxpr/ppermute | solution.py:24
  104.1 8.9 %collective-permute-start.1 = (bf16[256,128]{1,0:T(8,128)(2,1)S(1)}, bf16[256,128]{1,0:T(8,128)(2,1)S(1)}, u32[]{:S(2)}, u32[]{:S(2)}) collective-permute-start(bf16[256,128]{1,0:T(8,128)(2,1)S(1)} %get-tuple-element.375), channel_id=1, source_target_pairs={{0,16},{16,32},{32,48},{48,64},{64,80},{80,96},{96,112},{112,128},... | collective-permute-start | bytes 196616 | tf_op jit(solution)/shard_map/while/body/eval_jaxpr/ppermute | solution.py:24
  113.1 8.3 %collective-permute-start = (bf16[256,128]{1,0:T(8,128)(2,1)S(1)}, bf16[256,128]{1,0:T(8,128)(2,1)S(1)}, u32[]{:S(2)}, u32[]{:S(2)}) collective-permute-start(bf16[256,128]{1,0:T(8,128)(2,1)S(1)} %get-tuple-element.374), channel_id=1, source_target_pairs={{0,16},{16,32},{32,48},{48,64},{64,80},{80,96},{96,112},{112,128},... | collective-permute-start | bytes 196616 | tf_op jit(solution)/shard_map/while/body/eval_jaxpr/ppermute | solution.py:24
  115.0 8.3 %collective-permute-start.1 = (bf16[256,128]{1,0:T(8,128)(2,1)S(1)}, bf16[256,128]{1,0:T(8,128)(2,1)S(1)}, u32[]{:S(2)}, u32[]{:S(2)}) collective-permute-start(bf16[256,128]{1,0:T(8,128)(2,1)S(1)} %get-tuple-element.375), channel_id=1, source_target_pairs={{0,16},{16,32},{32,48},{48,64},{64,80},{80,96},{96,112},{112,128},... | collective-permute-start | bytes 196616 | tf_op jit(solution)/shard_map/while/body/eval_jaxpr/ppermute | solution.py:24
  123.3 8.9 %collective-permute-start = (bf16[256,128]{1,0:T(8,128)(2,1)S(1)}, bf16[256,128]{1,0:T(8,128)(2,1)S(1)}, u32[]{:S(2)}, u32[]{:S(2)}) collective-permute-start(bf16[256,128]{1,0:T(8,128)(2,1)S(1)} %get-tuple-element.374), channel_id=1, source_target_pairs={{0,16},{16,32},{32,48},{48,64},{64,80},{80,96},{96,112},{112,128},... | collective-permute-start | bytes 196616 | tf_op jit(solution)/shard_map/while/body/eval_jaxpr/ppermute | solution.py:24
  125.3 8.3 %collective-permute-start.1 = (bf16[256,128]{1,0:T(8,128)(2,1)S(1)}, bf16[256,128]{1,0:T(8,128)(2,1)S(1)}, u32[]{:S(2)}, u32[]{:S(2)}) collective-permute-start(bf16[256,128]{1,0:T(8,128)(2,1)S(1)} %get-tuple-element.375), channel_id=1, source_target_pairs={{0,16},{16,32},{32,48},{48,64},{64,80},{80,96},{96,112},{112,128},... | collective-permute-start | bytes 196616 | tf_op jit(solution)/shard_map/while/body/eval_jaxpr/ppermute | solution.py:24
  133.6 8.7 %collective-permute-start = (bf16[256,128]{1,0:T(8,128)(2,1)S(1)}, bf16[256,128]{1,0:T(8,128)(2,1)S(1)}, u32[]{:S(2)}, u32[]{:S(2)}) collective-permute-start(bf16[256,128]{1,0:T(8,128)(2,1)S(1)} %get-tuple-element.374), channel_id=1, source_target_pairs={{0,16},{16,32},{32,48},{48,64},{64,80},{80,96},{96,112},{112,128},... | collective-permute-start | bytes 196616 | tf_op jit(solution)/shard_map/while/body/eval_jaxpr/ppermute | solution.py:24
  135.5 8.3 %collective-permute-start.1 = (bf16[256,128]{1,0:T(8,128)(2,1)S(1)}, bf16[256,128]{1,0:T(8,128)(2,1)S(1)}, u32[]{:S(2)}, u32[]{:S(2)}) collective-permute-start(bf16[256,128]{1,0:T(8,128)(2,1)S(1)} %get-tuple-element.375), channel_id=1, source_target_pairs={{0,16},{16,32},{32,48},{48,64},{64,80},{80,96},{96,112},{112,128},... | collective-permute-start | bytes 196616 | tf_op jit(solution)/shard_map/while/body/eval_jaxpr/ppermute | solution.py:24
  143.8 8.3 %collective-permute-start = (bf16[256,128]{1,0:T(8,128)(2,1)S(1)}, bf16[256,128]{1,0:T(8,128)(2,1)S(1)}, u32[]{:S(2)}, u32[]{:S(2)}) collective-permute-start(bf16[256,128]{1,0:T(8,128)(2,1)S(1)} %get-tuple-element.374), channel_id=1, source_target_pairs={{0,16},{16,32},{32,48},{48,64},{64,80},{80,96},{96,112},{112,128},... | collective-permute-start | bytes 196616 | tf_op jit(solution)/shard_map/while/body/eval_jaxpr/ppermute | solution.py:24
  145.8 8.3 %collective-permute-start.1 = (bf16[256,128]{1,0:T(8,128)(2,1)S(1)}, bf16[256,128]{1,0:T(8,128)(2,1)S(1)}, u32[]{:S(2)}, u32[]{:S(2)}) collective-permute-start(bf16[256,128]{1,0:T(8,128)(2,1)S(1)} %get-tuple-element.375), channel_id=1, source_target_pairs={{0,16},{16,32},{32,48},{48,64},{64,80},{80,96},{96,112},{112,128},... | collective-permute-start | bytes 196616 | tf_op jit(solution)/shard_map/while/body/eval_jaxpr/ppermute | solution.py:24
  154.1 8.3 %collective-permute-start = (bf16[256,128]{1,0:T(8,128)(2,1)S(1)}, bf16[256,128]{1,0:T(8,128)(2,1)S(1)}, u32[]{:S(2)}, u32[]{:S(2)}) collective-permute-start(bf16[256,128]{1,0:T(8,128)(2,1)S(1)} %get-tuple-element.374), channel_id=1, source_target_pairs={{0,16},{16,32},{32,48},{48,64},{64,80},{80,96},{96,112},{112,128},... | collective-permute-start | bytes 196616 | tf_op jit(solution)/shard_map/while/body/eval_jaxpr/ppermute | solution.py:24
  156.0 8.3 %collective-permute-start.1 = (bf16[256,128]{1,0:T(8,128)(2,1)S(1)}, bf16[256,128]{1,0:T(8,128)(2,1)S(1)}, u32[]{:S(2)}, u32[]{:S(2)}) collective-permute-start(bf16[256,128]{1,0:T(8,128)(2,1)S(1)} %get-tuple-element.375), channel_id=1, source_target_pairs={{0,16},{16,32},{32,48},{48,64},{64,80},{80,96},{96,112},{112,128},... | collective-permute-start | bytes 196616 | tf_op jit(solution)/shard_map/while/body/eval_jaxpr/ppermute | solution.py:24
  164.3 8.3 %collective-permute-start = (bf16[256,128]{1,0:T(8,128)(2,1)S(1)}, bf16[256,128]{1,0:T(8,128)(2,1)S(1)}, u32[]{:S(2)}, u32[]{:S(2)}) collective-permute-start(bf16[256,128]{1,0:T(8,128)(2,1)S(1)} %get-tuple-element.374), channel_id=1, source_target_pairs={{0,16},{16,32},{32,48},{48,64},{64,80},{80,96},{96,112},{112,128},... | collective-permute-start | bytes 196616 | tf_op jit(solution)/shard_map/while/body/eval_jaxpr/ppermute | solution.py:24
  166.3 8.3 %collective-permute-start.1 = (bf16[256,128]{1,0:T(8,128)(2,1)S(1)}, bf16[256,128]{1,0:T(8,128)(2,1)S(1)}, u32[]{:S(2)}, u32[]{:S(2)}) collective-permute-start(bf16[256,128]{1,0:T(8,128)(2,1)S(1)} %get-tuple-element.375), channel_id=1, source_target_pairs={{0,16},{16,32},{32,48},{48,64},{64,80},{80,96},{96,112},{112,128},... | collective-permute-start | bytes 196616 | tf_op jit(solution)/shard_map/while/body/eval_jaxpr/ppermute | solution.py:24
  174.6 8.3 %collective-permute-start = (bf16[256,128]{1,0:T(8,128)(2,1)S(1)}, bf16[256,128]{1,0:T(8,128)(2,1)S(1)}, u32[]{:S(2)}, u32[]{:S(2)}) collective-permute-start(bf16[256,128]{1,0:T(8,128)(2,1)S(1)} %get-tuple-element.374), channel_id=1, source_target_pairs={{0,16},{16,32},{32,48},{48,64},{64,80},{80,96},{96,112},{112,128},... | collective-permute-start | bytes 196616 | tf_op jit(solution)/shard_map/while/body/eval_jaxpr/ppermute | solution.py:24
  176.5 8.3 %collective-permute-start.1 = (bf16[256,128]{1,0:T(8,128)(2,1)S(1)}, bf16[256,128]{1,0:T(8,128)(2,1)S(1)}, u32[]{:S(2)}, u32[]{:S(2)}) collective-permute-start(bf16[256,128]{1,0:T(8,128)(2,1)S(1)} %get-tuple-element.375), channel_id=1, source_target_pairs={{0,16},{16,32},{32,48},{48,64},{64,80},{80,96},{96,112},{112,128},... | collective-permute-start | bytes 196616 | tf_op jit(solution)/shard_map/while/body/eval_jaxpr/ppermute | solution.py:24
  251.5 6.6 %collective-permute-start.11 = (bf16[640,128]{1,0:T(8,128)(2,1)}, bf16[640,128]{1,0:T(8,128)(2,1)}, u32[]{:S(2)}, u32[]{:S(2)}) collective-permute-start(bf16[640,128]{1,0:T(8,128)(2,1)} %collective-permute-done.10), channel_id=1, source_target_pairs={{0,1},{1,2},{2,3},{3,4},{4,5},{5,6},{6,7},{7,8},{8,9},{9,10},{10,1... | collective-permute-start | bytes 491528 | tf_op jit(solution)/shard_map/ppermute | solution.py:15
  252.6 14.8 %all-to-all-start = ((bf16[32,20,128]{2,1,0:T(8,128)(2,1)}), bf16[32,20,128]{2,1,0:T(8,128)(2,1)S(1)}, u32[]{:S(2)}, u32[]{:S(2)}) async-start(bf16[32,20,128]{2,1,0:T(8,128)(2,1)} %all_to_all.24), calls=%async_computation | async-start | bytes 393216 | tf_op jit(solution)/shard_map/all_to_all | solution.py:114
  258.0 65.7 %all-gather.2.cloned.1.call-start = ((), (), s32[]{:S(2)}) async-start(), calls=%async_computation.4 | async-start | bytes 2785280 | tf_op jit(solution)/shard_map/all_gather | solution.py:120
  268.1 131.6 %reduce-scatter.4.cloned.1.call-start = ((), (), s32[]{:S(2)}) async-start(), calls=%async_computation.5 | async-start | bytes 2785280
  283.4 7.7 %collective-permute-start.16 = (bf16[640,128]{1,0:T(8,128)(2,1)S(1)}, bf16[640,128]{1,0:T(8,128)(2,1)S(1)}, u32[]{:S(2)}, u32[]{:S(2)}) collective-permute-start(bf16[640,128]{1,0:T(8,128)(2,1)S(1)} %collective-permute-done.15), channel_id=1, source_target_pairs={{0,1},{1,2},{2,3},{3,4},{4,5},{5,6},{6,7},{7,8},{8,9},{9,10},{10,1... | collective-permute-start | bytes 491528 | tf_op jit(solution)/shard_map/ppermute | solution.py:15
  291.8 6.9 %collective-permute-start.17 = (bf16[640,128]{1,0:T(8,128)(2,1)S(1)}, bf16[640,128]{1,0:T(8,128)(2,1)}, u32[]{:S(2)}, u32[]{:S(2)}) collective-permute-start(bf16[640,128]{1,0:T(8,128)(2,1)S(1)} %collective-permute-done.16), channel_id=1, source_target_pairs={{0,1},{1,2},{2,3},{3,4},{4,5},{5,6},{6,7},{7,8},{8,9},{9,10},{10,1... | collective-permute-start | bytes 491528 | tf_op jit(solution)/shard_map/ppermute | solution.py:15
  298.8 7.0 %collective-permute-start.18 = (bf16[640,128]{1,0:T(8,128)(2,1)}, bf16[640,128]{1,0:T(8,128)(2,1)}, u32[]{:S(2)}, u32[]{:S(2)}) collective-permute-start(bf16[640,128]{1,0:T(8,128)(2,1)} %collective-permute-done.17), channel_id=1, source_target_pairs={{0,1},{1,2},{2,3},{3,4},{4,5},{5,6},{6,7},{7,8},{8,9},{9,10},{10,1... | collective-permute-start | bytes 491528 | tf_op jit(solution)/shard_map/ppermute | solution.py:15
  401.5 19.9 %all-to-all-start.2 = ((bf16[128,32,20]{0,2,1:T(8,128)(2,1)}), bf16[128,32,20]{0,2,1:T(8,128)(2,1)S(1)}, u32[]{:S(2)}, u32[]{:S(2)}) async-start(bf16[128,32,20]{0,2,1:T(8,128)(2,1)} %all_to_all.30), calls=%async_computation.2 | async-start | bytes 393216 | tf_op jit(solution)/shard_map/all_to_all | solution.py:141
  436.7 6.9 %collective-permute-start.2 = (bf16[256,128]{1,0:T(8,128)(2,1)S(1)}, bf16[256,128]{1,0:T(8,128)(2,1)S(1)}, u32[]{:S(2)}, u32[]{:S(2)}) collective-permute-start(bf16[256,128]{1,0:T(8,128)(2,1)S(1)} %get-tuple-element.397), channel_id=1, source_target_pairs={{16,0},{32,16},{48,32},{64,48},{80,64},{96,80},{112,96},{128,112},... | collective-permute-start | bytes 196616 | tf_op jit(solution)/shard_map/while/body/eval_jaxpr/ppermute | solution.py:24
  439.9 6.6 %collective-permute-start.3 = (bf16[256,128]{1,0:T(8,128)(2,1)S(1)}, bf16[256,128]{1,0:T(8,128)(2,1)S(1)}, u32[]{:S(2)}, u32[]{:S(2)}) collective-permute-start(bf16[256,128]{1,0:T(8,128)(2,1)S(1)} %get-tuple-element.398), channel_id=1, source_target_pairs={{16,0},{32,16},{48,32},{64,48},{80,64},{96,80},{112,96},{128,112},... | collective-permute-start | bytes 196616 | tf_op jit(solution)/shard_map/while/body/eval_jaxpr/ppermute | solution.py:24
  447.4 7.3 %collective-permute-start.2 = (bf16[256,128]{1,0:T(8,128)(2,1)S(1)}, bf16[256,128]{1,0:T(8,128)(2,1)S(1)}, u32[]{:S(2)}, u32[]{:S(2)}) collective-permute-start(bf16[256,128]{1,0:T(8,128)(2,1)S(1)} %get-tuple-element.397), channel_id=1, source_target_pairs={{16,0},{32,16},{48,32},{64,48},{80,64},{96,80},{112,96},{128,112},... | collective-permute-start | bytes 196616 | tf_op jit(solution)/shard_map/while/body/eval_jaxpr/ppermute | solution.py:24
  475.5 6.5 %collective-permute-start.3 = (bf16[256,128]{1,0:T(8,128)(2,1)S(1)}, bf16[256,128]{1,0:T(8,128)(2,1)S(1)}, u32[]{:S(2)}, u32[]{:S(2)}) collective-permute-start(bf16[256,128]{1,0:T(8,128)(2,1)S(1)} %get-tuple-element.398), channel_id=1, source_target_pairs={{16,0},{32,16},{48,32},{64,48},{80,64},{96,80},{112,96},{128,112},... | collective-permute-start | bytes 196616 | tf_op jit(solution)/shard_map/while/body/eval_jaxpr/ppermute | solution.py:24
  527.3 6.6 %collective-permute-start.2 = (bf16[256,128]{1,0:T(8,128)(2,1)S(1)}, bf16[256,128]{1,0:T(8,128)(2,1)S(1)}, u32[]{:S(2)}, u32[]{:S(2)}) collective-permute-start(bf16[256,128]{1,0:T(8,128)(2,1)S(1)} %get-tuple-element.397), channel_id=1, source_target_pairs={{16,0},{32,16},{48,32},{64,48},{80,64},{96,80},{112,96},{128,112},... | collective-permute-start | bytes 196616 | tf_op jit(solution)/shard_map/while/body/eval_jaxpr/ppermute | solution.py:24
  542.5 6.4 %collective-permute-start.3 = (bf16[256,128]{1,0:T(8,128)(2,1)S(1)}, bf16[256,128]{1,0:T(8,128)(2,1)S(1)}, u32[]{:S(2)}, u32[]{:S(2)}) collective-permute-start(bf16[256,128]{1,0:T(8,128)(2,1)S(1)} %get-tuple-element.398), channel_id=1, source_target_pairs={{16,0},{32,16},{48,32},{64,48},{80,64},{96,80},{112,96},{128,112},... | collective-permute-start | bytes 196616 | tf_op jit(solution)/shard_map/while/body/eval_jaxpr/ppermute | solution.py:24
  583.2 6.7 %collective-permute-start.2 = (bf16[256,128]{1,0:T(8,128)(2,1)S(1)}, bf16[256,128]{1,0:T(8,128)(2,1)S(1)}, u32[]{:S(2)}, u32[]{:S(2)}) collective-permute-start(bf16[256,128]{1,0:T(8,128)(2,1)S(1)} %get-tuple-element.397), channel_id=1, source_target_pairs={{16,0},{32,16},{48,32},{64,48},{80,64},{96,80},{112,96},{128,112},... | collective-permute-start | bytes 196616 | tf_op jit(solution)/shard_map/while/body/eval_jaxpr/ppermute | solution.py:24
  587.2 6.7 %collective-permute-start.3 = (bf16[256,128]{1,0:T(8,128)(2,1)S(1)}, bf16[256,128]{1,0:T(8,128)(2,1)S(1)}, u32[]{:S(2)}, u32[]{:S(2)}) collective-permute-start(bf16[256,128]{1,0:T(8,128)(2,1)S(1)} %get-tuple-element.398), channel_id=1, source_target_pairs={{16,0},{32,16},{48,32},{64,48},{80,64},{96,80},{112,96},{128,112},... | collective-permute-start | bytes 196616 | tf_op jit(solution)/shard_map/while/body/eval_jaxpr/ppermute | solution.py:24
  (53 other events, 730.8 us)
Sparse Core Ops, SparseCore 0:
  268.2 44.3 all-gather.1
  333.6 66.0 reduce-scatter.3
